TPU v7x, 32 devices: a whole 2x2x4 slice. The times are simulated.
32 devices in a mesh: seq: 16 (over z, y, x), head: 2 (over core).
Axes of the slice: x: 2, y: 2, z: 4, core: 2. Of those that a mesh axis runs over, the one named last changes fastest.
Arguments:
- queries: bfloat16 [4096, 5120], P('seq', 'head'), may hold values from -100 to 100
- keys: bfloat16 [4096, 5120], P('seq', 'head'), may hold values from -12 to 12
- values: bfloat16 [4096, 5120], P('seq', 'head'), may hold values from -6 to 6
- hidden: bfloat16 [4096, 5120], P('seq', 'head'), may hold values from -3 to 3
- cached: bfloat16 [4096, 5120], P('seq', 'head'), may hold values from -6 to 6
- active: int32 [4096], P('seq'), may hold values from 0 to 1, as said below
- w_out: bfloat16 [5120, 5120], P('head', 'seq'), may hold values from -0.078125 to 0.078125
Outputs:
- block_output: bfloat16 [4096, 5120], P('seq', 'head')
Inputs may be any that keep to these rules, and one draw needn't show every extreme that they name: `active`: exactly 176 ones in all; among the 256 tokens of one index of seq at most 32 ones, and that many on some of them.
All inputs are finite; a program needn't handle non-finite values.
Results may differ from a plain program's by a relative error of at most 0.0039.
Values may be sent and summed in bfloat16 or wider, within the bound.
No kernel may reach another device: no remote copies, remote signals or barrier semaphores. Data moves between devices by JAX's collectives and lax.ppermute only.
A program may use at most 64 MiB of HBM per device.

v0:
```python
import jax
import jax.numpy as jnp
from jax import lax
from jax.sharding import PartitionSpec as P

HD = 128


def for_sending(value):

    def short(part):
        return part.astype(jnp.bfloat16) if part.dtype == jnp.float32 else part

    return jax.tree.map(short, value)


def local_partials(query_rows, keys, values):
    head_count = keys.shape[1] // HD
    inv_root = 1.0 / HD**0.5

    def one_head(head):
        start = head * HD
        q_head = lax.dynamic_slice_in_dim(query_rows, start, HD, 1)
        k_head = lax.dynamic_slice_in_dim(keys, start, HD, 1)
        v_head = lax.dynamic_slice_in_dim(values, start, HD, 1)
        scores = (
            lax.dot_general(
                q_head, k_head, (((1,), (1,)), ((), ())), preferred_element_type=jnp.float32
            )
            * inv_root
        )
        peak = jnp.max(scores, axis=1)
        expo = jnp.exp(scores - peak[:, None])
        total = jnp.sum(expo, axis=1)
        block_out = jnp.dot(expo.astype(jnp.bfloat16), v_head, preferred_element_type=jnp.float32)
        return ((block_out / total[:, None]).astype(jnp.bfloat16), peak, total)

    return lax.map(one_head, jnp.arange(head_count, dtype=jnp.int32))


def shards(queries, keys, values, hidden, cached, active, w_out):
    tok_dev, features = queries.shape
    head_count = features // HD
    devices = lax.axis_size("seq")
    capacity = tok_dev // 8
    act_rows = jnp.nonzero(active, size=capacity, fill_value=tok_dev)[0].astype(jnp.int32)
    safe_rows = jnp.minimum(act_rows, tok_dev - 1)
    own_queries = queries[safe_rows]
    gathered = lax.all_gather(own_queries, "seq", axis=0, tiled=True)
    block_out, block_peak, block_total = local_partials(gathered, keys, values)
    block_out = block_out.reshape(head_count, devices, capacity, HD)
    peak_in, total_in = (
        lax.all_to_all(
            block_peak.reshape(head_count, devices, capacity),
            "seq",
            split_axis=1,
            concat_axis=1,
            tiled=True,
        ),
        lax.all_to_all(
            block_total.reshape(head_count, devices, capacity),
            "seq",
            split_axis=1,
            concat_axis=1,
            tiled=True,
        ),
    )
    out_in = lax.all_to_all(
        for_sending(block_out), "seq", split_axis=1, concat_axis=1, tiled=True
    ).astype(block_out.dtype)
    top_max = jnp.max(peak_in, axis=1, keepdims=True)
    weight = total_in * jnp.exp(peak_in - top_max)
    mixed = jnp.einsum("hnc,hncd->hcd", weight, out_in.astype(jnp.float32))
    mixed = mixed / jnp.sum(weight, axis=1)[:, :, None]
    attn = jnp.transpose(mixed, (1, 0, 2)).reshape(capacity, features).astype(jnp.bfloat16)
    own_columns = w_out.shape[1]
    terms = jnp.dot(
        lax.all_gather(attn, "seq", axis=0, tiled=True), w_out, preferred_element_type=jnp.float32
    )
    terms = lax.psum(terms.astype(jnp.bfloat16), "head").astype(jnp.float32)
    terms = terms.reshape(devices, capacity, own_columns)
    arrived = lax.all_to_all(
        terms.astype(jnp.bfloat16), "seq", split_axis=0, concat_axis=2, tiled=True
    ).astype(terms.dtype)
    summed = lax.dynamic_slice_in_dim(arrived[0], lax.axis_index("head") * features, features, 1)
    updated = (hidden[safe_rows].astype(jnp.float32) + summed).astype(jnp.bfloat16)
    return cached.at[act_rows].set(updated, mode="drop")


def solution(mesh):
    placed = (
        P("seq", "head"),
        P("seq", "head"),
        P("seq", "head"),
        P("seq", "head"),
        P("seq", "head"),
        P("seq"),
        P("head", "seq"),
    )
    return jax.shard_map(
        shards, mesh=mesh, in_specs=placed, out_specs=P("seq", "head"), check_vma=False
    )
```

profile of v0, /device:TPU:0, one launch (start us, length us, event | category | flops | bytes accessed | tf_op | source)
XLA Modules:
  0.0 377.9 jit_solution(9547690487952534565)
XLA Ops:
  6.5 2.6 copy.57
  10.5 2.3 scatter_custom_fusion
  15.2 66.8 %all-gather.6.cloned.1.call-done = bf16[512,2560]{1,0:T(8,128)(2,1)} async-done(((bf16[32,2560]{1,0:T(8,128)(2,1)}), bf16[512,2560]{1,0:T(8,128)(2,1)}) %all-gather.6.cloned.1.call-update) | async-done | bytes 2621456 | tf_op jit(solution)/shard_map/all_gather | solution.py:49
  82.0 88.6 %while.14 = (s32[]{:T(128)}, bf16[20,512,128]{2,1,0:T(8,128)(2,1)}, f32[20,512]{1,0:T(8,128)S(1)}, f32[20,512]{1,0:T(8,128)S(1)}, s32[20]{0:T(128)S(1)}, /*index...) while((s32[]{:T(128)}, bf16[20,512,128]{2,1,0:T(8,128)(2,1)}, ...), condition=%wide.region_8.9_spmd, body=%wide.region_5.8_spmd.sunk | while | flops 68025344 | bytes 1986235 | solution.py:38
  89.0 1.8 fusion.42
  93.4 1.8 fusion.42
  97.8 1.8 fusion.42
  102.3 1.8 fusion.42
  106.7 1.8 fusion.42
  111.1 1.8 fusion.42
  124.4 1.8 fusion.42
  133.3 1.8 fusion.42
  146.5 1.8 fusion.42
  151.0 1.8 fusion.42
  155.4 1.8 fusion.42
  159.8 1.8 fusion.42
  164.3 1.8 fusion.42
  168.7 1.8 fusion.42
  171.5 4.1 %all-to-all-start.2 = ((f32[16,1,640]{2,1,0:T(1,128)}), f32[16,1,640]{2,1,0:T(1,128)S(1)}, u32[]{:S(2)}, u32[]{:S(2)}) async-start(f32[16,1,640]{2,1,0:T(1,128)} %reshape.215), calls=%async_computation.2 | async-start | bytes 81920 | tf_op jit(solution)/shard_map/all_to_all | solution.py:53
  176.5 6.5 %all-to-all-done.2 = f32[16,1,640]{2,1,0:T(1,128)S(1)} async-done(((f32[16,1,640]{2,1,0:T(1,128)}), f32[16,1,640]{2,1,0:T(1,128)S(1)}, u32[]{:S(2)}, u32[]{:S(2)}) %all-to-all-start.2) | async-done | bytes 40992 | tf_op jit(solution)/shard_map/all_to_all | solution.py:53
  183.1 3.5 all-to-all-start.1
  186.6 3.9 %copy.18 = bf16[20,16,32,128]{3,2,0,1:T(8,128)(2,1)} copy(bf16[20,16,32,128]{3,2,1,0:T(8,128)(2,1)} %bitcast.61) | data formatting | bytes 5242880 | tf_op jit(solution)/shard_map/reshape | solution.py:51
  190.5 3.5 all-to-all-done.1
  194.0 4.4 %all-to-all-start = ((bf16[20,16,32,128]{3,2,0,1:T(8,128)(2,1)}), bf16[20,16,32,128]{3,2,0,1:T(8,128)(2,1)}, u32[]{:S(2)}, u32[]{:S(2)}) async-start(bf16[20,16,32,128]{3,2,0,1:T(8,128)(2,1)} %copy.18), calls=%async_computation | async-start | bytes 5242880 | tf_op jit(solution)/shard_map/all_to_all | solution.py:68
  201.1 46.9 %all-to-all-done = bf16[20,16,32,128]{3,2,0,1:T(8,128)(2,1)} async-done(((bf16[20,16,32,128]{3,2,0,1:T(8,128)(2,1)}), bf16[20,16,32,128]{3,2,0,1:T(8,128)(2,1)}, u32[]{:S(2)}, u32[]{:S(2)}) %all-to-all-start) | async-done | bytes 2621472 | tf_op jit(solution)/shard_map/all_to_all | solution.py:68
  248.0 4.9 %fusion.12 = f32[32,20,1,128]{3,2,1,0:T(1,128)S(1)} fusion(bf16[20,16,32,1]{1,3,0,2:T(2,128)(2,1)S(1)} %copy.26, bf16[20,16,32,128]{3,2,0,1:T(8,128)(2,1)} %all-to-all-done), kind=kOutput, calls=%fused_computation.18 | convolution fusion | flops 2621440 | bytes 2969600 | tf_op jit(solution)/shard_map/hnc,hncd->hcd/dot_general | solution.py:73
  253.9 70.8 %all-gather.4.cloned.1.call-done = bf16[512,2560]{1,0:T(8,128)(2,1)} async-done(((bf16[32,2560]{1,0:T(8,128)(2,1)}), bf16[512,2560]{1,0:T(8,128)(2,1)}) %all-gather.4.cloned.1.call-update) | async-done | bytes 2621456 | tf_op jit(solution)/shard_map/all_gather | solution.py:78
  324.7 2.8 convolution_convert_fusion
  328.4 17.1 %all-reduce.2.cloned.1.call-done = bf16[16,32,320]{2,1,0:T(8,128)(2,1)} async-done(((bf16[16,32,320]{2,1,0:T(8,128)(2,1)}), bf16[16,32,320]{2,1,0:T(8,128)(2,1)}) %all-reduce.2.cloned.1.call-update) | async-done | bytes 327696 | tf_op jit(solution)/shard_map/psum | solution.py:80
  345.5 6.8 %all-to-all-start.3 = ((bf16[16,32,320]{2,1,0:T(8,128)(2,1)}), bf16[16,32,320]{2,1,0:T(8,128)(2,1)S(1)}, u32[]{:S(2)}, u32[]{:S(2)}) async-start(bf16[16,32,320]{2,1,0:T(8,128)(2,1)} %all-reduce.2.cloned.1.call-done), calls=%async_computation.3 | async-start | bytes 786432 | tf_op jit(solution)/shard_map/all_to_all | solution.py:82
  352.3 13.0 %all-to-all-done.3 = bf16[16,32,320]{2,1,0:T(8,128)(2,1)S(1)} async-done(((bf16[16,32,320]{2,1,0:T(8,128)(2,1)}), bf16[16,32,320]{2,1,0:T(8,128)(2,1)S(1)}, u32[]{:S(2)}, u32[]{:S(2)}) %all-to-all-start.3) | async-done | bytes 327712 | tf_op jit(solution)/shard_map/all_to_all | solution.py:82
  366.1 5.3 %scatter_custom_fusion.1 = bf16[256,2560]{1,0:T(8,128)(2,1)} fusion(bf16[256,2560]{1,0:T(8,128)(2,1)} %copy.57, s32[32]{0:T(128)S(1)} %get-tuple-element.53, f32[1,32,5120]{2,1,0:T(8,128)S(1)} %reshape.161, s32[]{:T(128)} %constant.71.clone.1, s32[]{:T(128)S(6)} %select_n.87, bf16[256,2560]{1,0:T(8,128)(2,1)} %param.12, s32[1024]{0:T(1024)S(1)} %pad_clamp_fusion), kind=kCustom, calls=%fused_computation.27 | custom fusion | flops 245760 | bytes 2953732 | tf_op jit(solution)/shard_map/scatter | solution.py:87
  (158 shorter events, 60.8 us)
Async XLA Ops:
  6.5 318.2 %copy-start = (bf16[2560,320]{0,1:T(8,128)(2,1)S(1)}, bf16[2560,320]{0,1:T(8,128)(2,1)}, u32[]{:S(2)}) copy-start(bf16[2560,320]{0,1:T(8,128)(2,1)} %param.15) | copy-start | bytes 4915204
  6.5 7.3 %copy-start.1 = (bf16[256,2560]{1,0:T(8,128)(2,1)S(1)}, bf16[256,2560]{1,0:T(8,128)(2,1)}, u32[]{:S(2)}) copy-start(bf16[256,2560]{1,0:T(8,128)(2,1)} %param.9) | copy-start | bytes 3932164
  6.5 2.6 copy-start.2
  6.5 75.5 %all-gather.6.cloned.1.call-start = ((), (), s32[]{:S(2)}) async-start(), calls=%async_computation.6 | async-start | bytes 2785280 | tf_op jit(solution)/shard_map/all_gather | solution.py:49
  171.5 11.6 %all-to-all-start.2 = ((f32[16,1,640]{2,1,0:T(1,128)}), f32[16,1,640]{2,1,0:T(1,128)S(1)}, u32[]{:S(2)}, u32[]{:S(2)}) async-start(f32[16,1,640]{2,1,0:T(1,128)} %reshape.215), calls=%async_computation.2 | async-start | bytes 81920 | tf_op jit(solution)/shard_map/all_to_all | solution.py:53
  183.1 10.9 %all-to-all-start.1 = ((f32[16,1,640]{2,1,0:T(1,128)}), f32[16,1,640]{2,1,0:T(1,128)S(1)}, u32[]{:S(2)}, u32[]{:S(2)}) async-start(f32[16,1,640]{2,1,0:T(1,128)} %reshape.213), calls=%async_computation.1 | async-start | bytes 81920 | tf_op jit(solution)/shard_map/all_to_all | solution.py:60
  194.0 54.0 %all-to-all-start = ((bf16[20,16,32,128]{3,2,0,1:T(8,128)(2,1)}), bf16[20,16,32,128]{3,2,0,1:T(8,128)(2,1)}, u32[]{:S(2)}, u32[]{:S(2)}) async-start(bf16[20,16,32,128]{3,2,0,1:T(8,128)(2,1)} %copy.18), calls=%async_computation | async-start | bytes 5242880 | tf_op jit(solution)/shard_map/all_to_all | solution.py:68
  198.4 126.3 %all-gather.4.cloned.1.call-start = ((), (), s32[]{:S(2)}) async-start(), calls=%async_computation.4 | async-start | bytes 2785280 | tf_op jit(solution)/shard_map/all_gather | solution.py:78
  253.8 91.7 %all-reduce.2.cloned.1.call-start = ((), (), s32[]{:S(2)}) async-start(), calls=%async_computation.5 | async-start | bytes 786432 | tf_op jit(solution)/shard_map/psum | solution.py:80
  345.5 19.8 %all-to-all-start.3 = ((bf16[16,32,320]{2,1,0:T(8,128)(2,1)}), bf16[16,32,320]{2,1,0:T(8,128)(2,1)S(1)}, u32[]{:S(2)}, u32[]{:S(2)}) async-start(bf16[16,32,320]{2,1,0:T(8,128)(2,1)} %all-reduce.2.cloned.1.call-done), calls=%async_computation.3 | async-start | bytes 786432 | tf_op jit(solution)/shard_map/all_to_all | solution.py:82
Sparse Core Ops, SparseCore 0:
  15.3 66.7 all-gather.5
  253.9 70.6 all-gather.3
  328.5 16.8 all-reduce.1
where the time goes:
time: 380 us; the launch traced here: 378 us
  waiting for transfers between devices  225 us (59%)
  matrix products  66.3 us (17%)
  local copies, waits for them, and re-layouts  27.4 us (7%)
  starting transfers between devices  19 us (5%)
  other arithmetic  13.7 us (4%)
  loops' own time  13.6 us (4%)
  between operations  13.3 us (4%)
    all_gather x1, waiting for transfers between devices, shards(): lax.all_gather(attn, 'seq', axis=0, tiled=True)  70.8 us
    all_gather x1, waiting for transfers between devices, shards(): gathered = lax.all_gather(own_queries, 'seq', axis=0, tiled=True)  66.8 us
    all_to_all x1, waiting for transfers between devices, shards(): lax.all_to_all(for_sending(block_out), 'seq', split_axis=1, concat_axis=1...  46.9 us
    dot_general x20, matrix products, one_head(): jnp.dot(expo.astype(jnp.bfloat16), v_head, preferred_element_type=jnp.flo...  35.6 us
    dot_general x20, matrix products, one_head(): lax.dot_general(q_head, k_head, (((1,), (1,)), ((), ())), preferred_eleme...  23 us
    psum x1, waiting for transfers between devices, shards(): terms = lax.psum(terms.astype(jnp.bfloat16), 'head').astype(jnp.float32)  17.1 us
    another operation x1, loops' own time, local_partials(): return lax.map(one_head, jnp.arange(head_count, dtype=jnp.int32))  13.6 us
    all_to_all x1, waiting for transfers between devices, shards(): lax.all_to_all(terms.astype(jnp.bfloat16), 'seq', split_axis=0, concat_ax...  13 us
  transfers between devices with their start and end apart: 7, of which 7 were waited for; matrix products, arithmetic and copies ran while one was open for 2% of the time, Pallas kernels for 0%

commit v1 on v0

--- a/solution.py
+++ b/solution.py
@@ -46,7 +46,12 @@
     act_rows = jnp.nonzero(active, size=capacity, fill_value=tok_dev)[0].astype(jnp.int32)
     safe_rows = jnp.minimum(act_rows, tok_dev - 1)
     own_queries = queries[safe_rows]
-    gathered = lax.all_gather(own_queries, "seq", axis=0, tiled=True)
+    ring = [own_queries]
+    for hop in range(15):
+        ring.append(lax.ppermute(ring[-1], "seq", [(dev, (dev + 1) % 16) for dev in range(16)]))
+    gathered = jnp.roll(
+        jnp.concatenate(ring[::-1], axis=0), (lax.axis_index("seq") + 1) * ring[0].shape[0], axis=0
+    )
     block_out, block_peak, block_total = local_partials(gathered, keys, values)
     block_out = block_out.reshape(head_count, devices, capacity, HD)
     peak_in, total_in = (

time: 380 us -> 452 us (1.19)
  waiting for transfers between devices: 225 us -> 276 us
  local copies, waits for them, and re-layouts: 27.4 us -> 39.7 us
  starting transfers between devices: 19 us -> 24.7 us
    ppermute x0 -> x15, waiting for transfers between devices: none -> 136 us  [shards(): lax.ppermute(ring[-1], 'seq', [(dev, (dev + 1) % 16) for dev in range(16)])]
    all_gather x1 -> x0, waiting for transfers between devices: 66.8 us -> none  [shards(): gathered = lax.all_gather(own_queries, 'seq', axis=0, tiled=True)]
    all_to_all x1, waiting for transfers between devices: 46.9 us -> 33.2 us  [shards(): lax.all_to_all(for_sending(block_out), 'seq', split_axis=1, concat_axis=1...]
    unnamed x12 -> x51, local copies, waits for them, and re-layouts: 4.98 us -> 13.7 us
  transfers between devices with their start and end apart: 7 -> 21, of which waited for: 7 -> 21; matrix products, arithmetic and copies ran while one was open for 2% -> 2% of each run, Pallas kernels for 0% -> 0%
where the time goes in v1:
time: 452 us; the launch traced here: 450 us
  waiting for transfers between devices  276 us (61%)
  matrix products  66.4 us (15%)
  local copies, waits for them, and re-layouts  39.7 us (9%)
  starting transfers between devices  24.7 us (5%)
  other arithmetic  15 us (3%)
  between operations  13.9 us (3%)
  loops' own time  13.6 us (3%)
    ppermute x15, waiting for transfers between devices, shards(): lax.ppermute(ring[-1], 'seq', [(dev, (dev + 1) % 16) for dev in range(16)])  136 us
    all_gather x1, waiting for transfers between devices, shards(): lax.all_gather(attn, 'seq', axis=0, tiled=True)  66.7 us
    dot_general x20, matrix products, one_head(): jnp.dot(expo.astype(jnp.bfloat16), v_head, preferred_element_type=jnp.flo...  35.6 us
    all_to_all x1, waiting for transfers between devices, shards(): lax.all_to_all(for_sending(block_out), 'seq', split_axis=1, concat_axis=1...  33.2 us
    dot_general x20, matrix products, one_head(): lax.dot_general(q_head, k_head, (((1,), (1,)), ((), ())), preferred_eleme...  23 us
    psum x1, waiting for transfers between devices, shards(): terms = lax.psum(terms.astype(jnp.bfloat16), 'head').astype(jnp.float32)  17 us
    unnamed x51, local copies, waits for them, and re-layouts  13.7 us
    another operation x1, loops' own time, local_partials(): return lax.map(one_head, jnp.arange(head_count, dtype=jnp.int32))  13.6 us
  transfers between devices with their start and end apart: 21, of which 21 were waited for; matrix products, arithmetic and copies ran while one was open for 2% of the time, Pallas kernels for 0%

profile of v1, /device:TPU:0, one launch (start us, length us, event | category | flops | bytes accessed | tf_op | source)
XLA Modules:
  0.0 449.5 jit_solution(14568617575904556824)
XLA Ops:
  6.5 2.6 copy.88
  17.4 3.0 collective-permute-start
  20.4 8.2 %collective-permute-done = bf16[32,2560]{1,0:T(8,128)(2,1)S(1)} collective-permute-done((bf16[32,2560]{1,0:T(8,128)(2,1)S(1)}, bf16[32,2560]{1,0:T(8,128)(2,1)S(1)}, u32[]{:S(2)}, u32[]{:S(2)}) %collective-permute-start) | collective-permute-done | bytes 163872 | tf_op jit(solution)/shard_map/ppermute | solution.py:51
  28.6 9.0 %collective-permute-done.1 = bf16[32,2560]{1,0:T(8,128)(2,1)S(1)} collective-permute-done((bf16[32,2560]{1,0:T(8,128)(2,1)S(1)}, bf16[32,2560]{1,0:T(8,128)(2,1)S(1)}, u32[]{:S(2)}, u32[]{:S(2)}) %collective-permute-start.1) | collective-permute-done | bytes 163872 | tf_op jit(solution)/shard_map/ppermute | solution.py:51
  37.6 8.9 %collective-permute-done.2 = bf16[32,2560]{1,0:T(8,128)(2,1)S(1)} collective-permute-done((bf16[32,2560]{1,0:T(8,128)(2,1)S(1)}, bf16[32,2560]{1,0:T(8,128)(2,1)S(1)}, u32[]{:S(2)}, u32[]{:S(2)}) %collective-permute-start.2) | collective-permute-done | bytes 163872 | tf_op jit(solution)/shard_map/ppermute | solution.py:51
  46.5 8.9 %collective-permute-done.3 = bf16[32,2560]{1,0:T(8,128)(2,1)S(1)} collective-permute-done((bf16[32,2560]{1,0:T(8,128)(2,1)S(1)}, bf16[32,2560]{1,0:T(8,128)(2,1)S(1)}, u32[]{:S(2)}, u32[]{:S(2)}) %collective-permute-start.3) | collective-permute-done | bytes 163872 | tf_op jit(solution)/shard_map/ppermute | solution.py:51
  55.4 8.9 %collective-permute-done.4 = bf16[32,2560]{1,0:T(8,128)(2,1)S(1)} collective-permute-done((bf16[32,2560]{1,0:T(8,128)(2,1)S(1)}, bf16[32,2560]{1,0:T(8,128)(2,1)S(1)}, u32[]{:S(2)}, u32[]{:S(2)}) %collective-permute-start.4) | collective-permute-done | bytes 163872 | tf_op jit(solution)/shard_map/ppermute | solution.py:51
  64.3 8.9 %collective-permute-done.5 = bf16[32,2560]{1,0:T(8,128)(2,1)S(1)} collective-permute-done((bf16[32,2560]{1,0:T(8,128)(2,1)S(1)}, bf16[32,2560]{1,0:T(8,128)(2,1)S(1)}, u32[]{:S(2)}, u32[]{:S(2)}) %collective-permute-start.5) | collective-permute-done | bytes 163872 | tf_op jit(solution)/shard_map/ppermute | solution.py:51
  73.2 10.1 %collective-permute-done.6 = bf16[32,2560]{1,0:T(8,128)(2,1)S(1)} collective-permute-done((bf16[32,2560]{1,0:T(8,128)(2,1)S(1)}, bf16[32,2560]{1,0:T(8,128)(2,1)S(1)}, u32[]{:S(2)}, u32[]{:S(2)}) %collective-permute-start.6) | collective-permute-done | bytes 163872 | tf_op jit(solution)/shard_map/ppermute | solution.py:51
  83.3 10.1 %collective-permute-done.7 = bf16[32,2560]{1,0:T(8,128)(2,1)S(1)} collective-permute-done((bf16[32,2560]{1,0:T(8,128)(2,1)S(1)}, bf16[32,2560]{1,0:T(8,128)(2,1)S(1)}, u32[]{:S(2)}, u32[]{:S(2)}) %collective-permute-start.7) | collective-permute-done | bytes 163872 | tf_op jit(solution)/shard_map/ppermute | solution.py:51
  93.4 9.3 %collective-permute-done.8 = bf16[32,2560]{1,0:T(8,128)(2,1)S(1)} collective-permute-done((bf16[32,2560]{1,0:T(8,128)(2,1)S(1)}, bf16[32,2560]{1,0:T(8,128)(2,1)S(1)}, u32[]{:S(2)}, u32[]{:S(2)}) %collective-permute-start.8) | collective-permute-done | bytes 163872 | tf_op jit(solution)/shard_map/ppermute | solution.py:51
  102.7 8.9 %collective-permute-done.9 = bf16[32,2560]{1,0:T(8,128)(2,1)S(1)} collective-permute-done((bf16[32,2560]{1,0:T(8,128)(2,1)S(1)}, bf16[32,2560]{1,0:T(8,128)(2,1)S(1)}, u32[]{:S(2)}, u32[]{:S(2)}) %collective-permute-start.9) | collective-permute-done | bytes 163872 | tf_op jit(solution)/shard_map/ppermute | solution.py:51
  111.6 8.9 %collective-permute-done.10 = bf16[32,2560]{1,0:T(8,128)(2,1)S(1)} collective-permute-done((bf16[32,2560]{1,0:T(8,128)(2,1)S(1)}, bf16[32,2560]{1,0:T(8,128)(2,1)S(1)}, u32[]{:S(2)}, u32[]{:S(2)}) %collective-permute-start.10) | collective-permute-done | bytes 163872 | tf_op jit(solution)/shard_map/ppermute | solution.py:51
  121.2 8.9 %collective-permute-done.11 = bf16[32,2560]{1,0:T(8,128)(2,1)S(1)} collective-permute-done((bf16[32,2560]{1,0:T(8,128)(2,1)S(1)}, bf16[32,2560]{1,0:T(8,128)(2,1)S(1)}, u32[]{:S(2)}, u32[]{:S(2)}) %collective-permute-start.11) | collective-permute-done | bytes 163872 | tf_op jit(solution)/shard_map/ppermute | solution.py:51
  130.8 8.9 %collective-permute-done.12 = bf16[32,2560]{1,0:T(8,128)(2,1)S(1)} collective-permute-done((bf16[32,2560]{1,0:T(8,128)(2,1)S(1)}, bf16[32,2560]{1,0:T(8,128)(2,1)S(1)}, u32[]{:S(2)}, u32[]{:S(2)}) %collective-permute-start.12) | collective-permute-done | bytes 163872 | tf_op jit(solution)/shard_map/ppermute | solution.py:51
  140.3 9.0 %collective-permute-done.13 = bf16[32,2560]{1,0:T(8,128)(2,1)} collective-permute-done((bf16[32,2560]{1,0:T(8,128)(2,1)S(1)}, bf16[32,2560]{1,0:T(8,128)(2,1)}, u32[]{:S(2)}, u32[]{:S(2)}) %collective-permute-start.13) | collective-permute-done | bytes 163872 | tf_op jit(solution)/shard_map/ppermute | solution.py:51
  149.4 9.2 %collective-permute-done.14 = bf16[32,2560]{1,0:T(8,128)(2,1)} collective-permute-done((bf16[32,2560]{1,0:T(8,128)(2,1)}, bf16[32,2560]{1,0:T(8,128)(2,1)}, u32[]{:S(2)}, u32[]{:S(2)}) %collective-permute-start.14) | collective-permute-done | bytes 163872 | tf_op jit(solution)/shard_map/ppermute | solution.py:51
  167.3 89.4 %while.14 = (s32[]{:T(128)}, bf16[20,512,128]{2,1,0:T(8,128)(2,1)}, f32[20,512]{1,0:T(8,128)S(1)}, f32[20,512]{1,0:T(8,128)S(1)}, s32[20]{0:T(128)S(1)}, /*index...) while((s32[]{:T(128)}, bf16[20,512,128]{2,1,0:T(8,128)(2,1)}, ...), condition=%wide.region_8.9_spmd, body=%wide.region_5.8_spmd.sunk | while | flops 68025344 | bytes 1986235 | solution.py:38
  257.7 3.5 all-to-all-start.2
  262.1 6.6 %all-to-all-done.2 = f32[16,1,640]{2,1,0:T(1,128)S(1)} async-done(((f32[16,1,640]{2,1,0:T(1,128)}), f32[16,1,640]{2,1,0:T(1,128)S(1)}, u32[]{:S(2)}, u32[]{:S(2)}) %all-to-all-start.2) | async-done | bytes 40992 | tf_op jit(solution)/shard_map/all_to_all | solution.py:58
  268.7 3.5 all-to-all-start.1
  272.2 3.9 copy.18
  276.1 3.6 all-to-all-done.1
  279.7 7.6 %all-to-all-start = ((bf16[20,16,32,128]{3,2,0,1:T(8,128)(2,1)}), bf16[20,16,32,128]{3,2,0,1:T(8,128)(2,1)}, u32[]{:S(2)}, u32[]{:S(2)}) async-start(bf16[20,16,32,128]{3,2,0,1:T(8,128)(2,1)} %copy.18), calls=%async_computation | async-start | bytes 5242880 | tf_op jit(solution)/shard_map/all_to_all | solution.py:73
  290.1 33.2 %all-to-all-done = bf16[20,16,32,128]{3,2,0,1:T(8,128)(2,1)} async-done(((bf16[20,16,32,128]{3,2,0,1:T(8,128)(2,1)}), bf16[20,16,32,128]{3,2,0,1:T(8,128)(2,1)}, u32[]{:S(2)}, u32[]{:S(2)}) %all-to-all-start) | async-done | bytes 2621472 | tf_op jit(solution)/shard_map/all_to_all | solution.py:73
  323.3 4.9 %fusion.12 = f32[32,20,1,128]{3,2,1,0:T(1,128)S(1)} fusion(bf16[20,16,32,1]{1,3,0,2:T(2,128)(2,1)S(1)} %copy.26, bf16[20,16,32,128]{3,2,0,1:T(8,128)(2,1)} %all-to-all-done), kind=kOutput, calls=%fused_computation.18 | convolution fusion | flops 2621440 | bytes 2969600 | tf_op jit(solution)/shard_map/hnc,hncd->hcd/dot_general | solution.py:78
  329.3 66.7 %all-gather.2.cloned.1.call-done = bf16[512,2560]{1,0:T(8,128)(2,1)} async-done(((bf16[32,2560]{1,0:T(8,128)(2,1)}), bf16[512,2560]{1,0:T(8,128)(2,1)}) %all-gather.2.cloned.1.call-update) | async-done | bytes 2621456 | tf_op jit(solution)/shard_map/all_gather | solution.py:83
  396.0 2.8 convolution_convert_fusion
  399.7 17.0 %all-reduce.2.cloned.1.call-done = bf16[16,32,320]{2,1,0:T(8,128)(2,1)} async-done(((bf16[16,32,320]{2,1,0:T(8,128)(2,1)}), bf16[16,32,320]{2,1,0:T(8,128)(2,1)}) %all-reduce.2.cloned.1.call-update) | async-done | bytes 327696 | tf_op jit(solution)/shard_map/psum | solution.py:85
  416.8 6.8 %all-to-all-start.3 = ((bf16[16,32,320]{2,1,0:T(8,128)(2,1)}), bf16[16,32,320]{2,1,0:T(8,128)(2,1)S(1)}, u32[]{:S(2)}, u32[]{:S(2)}) async-start(bf16[16,32,320]{2,1,0:T(8,128)(2,1)} %all-reduce.2.cloned.1.call-done), calls=%async_computation.3 | async-start | bytes 786432 | tf_op jit(solution)/shard_map/all_to_all | solution.py:87
  423.6 13.0 %all-to-all-done.3 = bf16[16,32,320]{2,1,0:T(8,128)(2,1)S(1)} async-done(((bf16[16,32,320]{2,1,0:T(8,128)(2,1)}), bf16[16,32,320]{2,1,0:T(8,128)(2,1)S(1)}, u32[]{:S(2)}, u32[]{:S(2)}) %all-to-all-start.3) | async-done | bytes 327712 | tf_op jit(solution)/shard_map/all_to_all | solution.py:87
  437.4 5.3 %scatter_custom_fusion.1 = bf16[256,2560]{1,0:T(8,128)(2,1)} fusion(bf16[256,2560]{1,0:T(8,128)(2,1)} %copy.88, s32[32]{0:T(128)S(1)} %get-tuple-element.53, f32[1,32,5120]{2,1,0:T(8,128)S(1)} %reshape.161, s32[]{:T(128)} %constant.93.clone.1, s32[]{:T(128)S(6)} %select_n.101, bf16[256,2560]{1,0:T(8,128)(2,1)} %param.12, s32[1024]{0:T(1024)S(1)} %pad_clamp_fusion), kind=kCustom, calls=%fused_computation.27 | custom fusion | flops 245760 | bytes 2953732 | tf_op jit(solution)/shard_map/scatter | solution.py:92
  (226 shorter events, 101.9 us)
Async XLA Ops:
  6.5 389.4 %copy-start = (bf16[2560,320]{0,1:T(8,128)(2,1)S(1)}, bf16[2560,320]{0,1:T(8,128)(2,1)}, u32[]{:S(2)}) copy-start(bf16[2560,320]{0,1:T(8,128)(2,1)} %param.15) | copy-start | bytes 4915204
  17.4 11.2 %collective-permute-start = (bf16[32,2560]{1,0:T(8,128)(2,1)S(1)}, bf16[32,2560]{1,0:T(8,128)(2,1)S(1)}, u32[]{:S(2)}, u32[]{:S(2)}) collective-permute-start(bf16[32,2560]{1,0:T(8,128)(2,1)S(1)} %gather_fusion), channel_id=1, source_target_pairs={{0,2},{2,4},{4,6},{6,8},{8,10},{10,12},{12,14},{14,16},{16,18},{18... | collective-permute-start | bytes 491528 | tf_op jit(solution)/shard_map/ppermute | solution.py:51
  28.6 9.0 %collective-permute-start.1 = (bf16[32,2560]{1,0:T(8,128)(2,1)S(1)}, bf16[32,2560]{1,0:T(8,128)(2,1)S(1)}, u32[]{:S(2)}, u32[]{:S(2)}) collective-permute-start(bf16[32,2560]{1,0:T(8,128)(2,1)S(1)} %collective-permute-done), channel_id=1, source_target_pairs={{0,2},{2,4},{4,6},{6,8},{8,10},{10,12},{12,14},{14,16},{16,18},{18... | collective-permute-start | bytes 491528 | tf_op jit(solution)/shard_map/ppermute | solution.py:51
  37.6 8.9 %collective-permute-start.2 = (bf16[32,2560]{1,0:T(8,128)(2,1)S(1)}, bf16[32,2560]{1,0:T(8,128)(2,1)S(1)}, u32[]{:S(2)}, u32[]{:S(2)}) collective-permute-start(bf16[32,2560]{1,0:T(8,128)(2,1)S(1)} %collective-permute-done.1), channel_id=1, source_target_pairs={{0,2},{2,4},{4,6},{6,8},{8,10},{10,12},{12,14},{14,16},{16,18},{18... | collective-permute-start | bytes 491528 | tf_op jit(solution)/shard_map/ppermute | solution.py:51
  46.5 8.9 %collective-permute-start.3 = (bf16[32,2560]{1,0:T(8,128)(2,1)S(1)}, bf16[32,2560]{1,0:T(8,128)(2,1)S(1)}, u32[]{:S(2)}, u32[]{:S(2)}) collective-permute-start(bf16[32,2560]{1,0:T(8,128)(2,1)S(1)} %collective-permute-done.2), channel_id=1, source_target_pairs={{0,2},{2,4},{4,6},{6,8},{8,10},{10,12},{12,14},{14,16},{16,18},{18... | collective-permute-start | bytes 491528 | tf_op jit(solution)/shard_map/ppermute | solution.py:51
  55.4 8.9 %collective-permute-start.4 = (bf16[32,2560]{1,0:T(8,128)(2,1)S(1)}, bf16[32,2560]{1,0:T(8,128)(2,1)S(1)}, u32[]{:S(2)}, u32[]{:S(2)}) collective-permute-start(bf16[32,2560]{1,0:T(8,128)(2,1)S(1)} %collective-permute-done.3), channel_id=1, source_target_pairs={{0,2},{2,4},{4,6},{6,8},{8,10},{10,12},{12,14},{14,16},{16,18},{18... | collective-permute-start | bytes 491528 | tf_op jit(solution)/shard_map/ppermute | solution.py:51
  64.3 8.9 %collective-permute-start.5 = (bf16[32,2560]{1,0:T(8,128)(2,1)S(1)}, bf16[32,2560]{1,0:T(8,128)(2,1)S(1)}, u32[]{:S(2)}, u32[]{:S(2)}) collective-permute-start(bf16[32,2560]{1,0:T(8,128)(2,1)S(1)} %collective-permute-done.4), channel_id=1, source_target_pairs={{0,2},{2,4},{4,6},{6,8},{8,10},{10,12},{12,14},{14,16},{16,18},{18... | collective-permute-start | bytes 491528 | tf_op jit(solution)/shard_map/ppermute | solution.py:51
  73.2 10.1 %collective-permute-start.6 = (bf16[32,2560]{1,0:T(8,128)(2,1)S(1)}, bf16[32,2560]{1,0:T(8,128)(2,1)S(1)}, u32[]{:S(2)}, u32[]{:S(2)}) collective-permute-start(bf16[32,2560]{1,0:T(8,128)(2,1)S(1)} %collective-permute-done.5), channel_id=1, source_target_pairs={{0,2},{2,4},{4,6},{6,8},{8,10},{10,12},{12,14},{14,16},{16,18},{18... | collective-permute-start | bytes 491528 | tf_op jit(solution)/shard_map/ppermute | solution.py:51
  83.3 10.1 %collective-permute-start.7 = (bf16[32,2560]{1,0:T(8,128)(2,1)S(1)}, bf16[32,2560]{1,0:T(8,128)(2,1)S(1)}, u32[]{:S(2)}, u32[]{:S(2)}) collective-permute-start(bf16[32,2560]{1,0:T(8,128)(2,1)S(1)} %collective-permute-done.6), channel_id=1, source_target_pairs={{0,2},{2,4},{4,6},{6,8},{8,10},{10,12},{12,14},{14,16},{16,18},{18... | collective-permute-start | bytes 491528 | tf_op jit(solution)/shard_map/ppermute | solution.py:51
  93.4 9.3 %collective-permute-start.8 = (bf16[32,2560]{1,0:T(8,128)(2,1)S(1)}, bf16[32,2560]{1,0:T(8,128)(2,1)S(1)}, u32[]{:S(2)}, u32[]{:S(2)}) collective-permute-start(bf16[32,2560]{1,0:T(8,128)(2,1)S(1)} %collective-permute-done.7), channel_id=1, source_target_pairs={{0,2},{2,4},{4,6},{6,8},{8,10},{10,12},{12,14},{14,16},{16,18},{18... | collective-permute-start | bytes 491528 | tf_op jit(solution)/shard_map/ppermute | solution.py:51
  102.7 8.9 %collective-permute-start.9 = (bf16[32,2560]{1,0:T(8,128)(2,1)S(1)}, bf16[32,2560]{1,0:T(8,128)(2,1)S(1)}, u32[]{:S(2)}, u32[]{:S(2)}) collective-permute-start(bf16[32,2560]{1,0:T(8,128)(2,1)S(1)} %collective-permute-done.8), channel_id=1, source_target_pairs={{0,2},{2,4},{4,6},{6,8},{8,10},{10,12},{12,14},{14,16},{16,18},{18... | collective-permute-start | bytes 491528 | tf_op jit(solution)/shard_map/ppermute | solution.py:51
  111.6 8.9 %collective-permute-start.10 = (bf16[32,2560]{1,0:T(8,128)(2,1)S(1)}, bf16[32,2560]{1,0:T(8,128)(2,1)S(1)}, u32[]{:S(2)}, u32[]{:S(2)}) collective-permute-start(bf16[32,2560]{1,0:T(8,128)(2,1)S(1)} %collective-permute-done.9), channel_id=1, source_target_pairs={{0,2},{2,4},{4,6},{6,8},{8,10},{10,12},{12,14},{14,16},{16,18},{18... | collective-permute-start | bytes 491528 | tf_op jit(solution)/shard_map/ppermute | solution.py:51
  120.5 0.7 copy-start.1
  121.2 8.9 %collective-permute-start.11 = (bf16[32,2560]{1,0:T(8,128)(2,1)S(1)}, bf16[32,2560]{1,0:T(8,128)(2,1)S(1)}, u32[]{:S(2)}, u32[]{:S(2)}) collective-permute-start(bf16[32,2560]{1,0:T(8,128)(2,1)S(1)} %collective-permute-done.10), channel_id=1, source_target_pairs={{0,2},{2,4},{4,6},{6,8},{8,10},{10,12},{12,14},{14,16},{16,18},{18... | collective-permute-start | bytes 491528 | tf_op jit(solution)/shard_map/ppermute | solution.py:51
  130.1 0.7 copy-start.3
  130.8 8.9 %collective-permute-start.12 = (bf16[32,2560]{1,0:T(8,128)(2,1)S(1)}, bf16[32,2560]{1,0:T(8,128)(2,1)S(1)}, u32[]{:S(2)}, u32[]{:S(2)}) collective-permute-start(bf16[32,2560]{1,0:T(8,128)(2,1)S(1)} %collective-permute-done.11), channel_id=1, source_target_pairs={{0,2},{2,4},{4,6},{6,8},{8,10},{10,12},{12,14},{14,16},{16,18},{18... | collective-permute-start | bytes 491528 | tf_op jit(solution)/shard_map/ppermute | solution.py:51
  139.7 0.7 copy-start.5
  140.3 9.0 %collective-permute-start.13 = (bf16[32,2560]{1,0:T(8,128)(2,1)S(1)}, bf16[32,2560]{1,0:T(8,128)(2,1)}, u32[]{:S(2)}, u32[]{:S(2)}) collective-permute-start(bf16[32,2560]{1,0:T(8,128)(2,1)S(1)} %collective-permute-done.12), channel_id=1, source_target_pairs={{0,2},{2,4},{4,6},{6,8},{8,10},{10,12},{12,14},{14,16},{16,18},{18... | collective-permute-start | bytes 491528 | tf_op jit(solution)/shard_map/ppermute | solution.py:51
  149.4 9.2 %collective-permute-start.14 = (bf16[32,2560]{1,0:T(8,128)(2,1)}, bf16[32,2560]{1,0:T(8,128)(2,1)}, u32[]{:S(2)}, u32[]{:S(2)}) collective-permute-start(bf16[32,2560]{1,0:T(8,128)(2,1)} %collective-permute-done.13), channel_id=1, source_target_pairs={{0,2},{2,4},{4,6},{6,8},{8,10},{10,12},{12,14},{14,16},{16,18},{18... | collective-permute-start | bytes 491528 | tf_op jit(solution)/shard_map/ppermute | solution.py:51
  149.4 16.0 %copy-start.6 = (bf16[32,2560]{1,0:T(8,128)(2,1)S(1)}, bf16[32,2560]{1,0:T(8,128)(2,1)}, u32[]{:S(2)}) copy-start(bf16[32,2560]{1,0:T(8,128)(2,1)} %copy-done.5) | copy-start | bytes 491524
  149.4 16.0 %copy-start.4 = (bf16[32,2560]{1,0:T(8,128)(2,1)S(1)}, bf16[32,2560]{1,0:T(8,128)(2,1)}, u32[]{:S(2)}) copy-start(bf16[32,2560]{1,0:T(8,128)(2,1)} %copy-done.3) | copy-start | bytes 491524
  149.4 16.0 %copy-start.2 = (bf16[32,2560]{1,0:T(8,128)(2,1)S(1)}, bf16[32,2560]{1,0:T(8,128)(2,1)}, u32[]{:S(2)}) copy-start(bf16[32,2560]{1,0:T(8,128)(2,1)} %copy-done.1) | copy-start | bytes 491524
  257.7 11.0 %all-to-all-start.2 = ((f32[16,1,640]{2,1,0:T(1,128)}), f32[16,1,640]{2,1,0:T(1,128)S(1)}, u32[]{:S(2)}, u32[]{:S(2)}) async-start(f32[16,1,640]{2,1,0:T(1,128)} %reshape.214), calls=%async_computation.2 | async-start | bytes 81920 | tf_op jit(solution)/shard_map/all_to_all | solution.py:58
  268.7 11.1 %all-to-all-start.1 = ((f32[16,1,640]{2,1,0:T(1,128)}), f32[16,1,640]{2,1,0:T(1,128)S(1)}, u32[]{:S(2)}, u32[]{:S(2)}) async-start(f32[16,1,640]{2,1,0:T(1,128)} %reshape.212), calls=%async_computation.1 | async-start | bytes 81920 | tf_op jit(solution)/shard_map/all_to_all | solution.py:65
  279.7 43.5 %all-to-all-start = ((bf16[20,16,32,128]{3,2,0,1:T(8,128)(2,1)}), bf16[20,16,32,128]{3,2,0,1:T(8,128)(2,1)}, u32[]{:S(2)}, u32[]{:S(2)}) async-start(bf16[20,16,32,128]{3,2,0,1:T(8,128)(2,1)} %copy.18), calls=%async_computation | async-start | bytes 5242880 | tf_op jit(solution)/shard_map/all_to_all | solution.py:73
  287.4 108.6 %all-gather.2.cloned.1.call-start = ((), (), s32[]{:S(2)}) async-start(), calls=%async_computation.4 | async-start | bytes 2785280 | tf_op jit(solution)/shard_map/all_gather | solution.py:83
  329.1 87.7 %all-reduce.2.cloned.1.call-start = ((), (), s32[]{:S(2)}) async-start(), calls=%async_computation.5 | async-start | bytes 786432 | tf_op jit(solution)/shard_map/psum | solution.py:85
  416.8 19.8 %all-to-all-start.3 = ((bf16[16,32,320]{2,1,0:T(8,128)(2,1)}), bf16[16,32,320]{2,1,0:T(8,128)(2,1)S(1)}, u32[]{:S(2)}, u32[]{:S(2)}) async-start(bf16[16,32,320]{2,1,0:T(8,128)(2,1)} %all-reduce.2.cloned.1.call-done), calls=%async_computation.3 | async-start | bytes 786432 | tf_op jit(solution)/shard_map/all_to_all | solution.py:87
Sparse Core Ops, SparseCore 0:
  329.2 66.7 all-gather.1
  399.8 16.8 all-reduce.1
